TPU v7x, 32 devices: a whole 2x2x4 slice. The times are simulated.
32 devices in a mesh: shard: 4 (over x, core), rep: 8 (over z, y).
Axes of the slice: x: 2, y: 2, z: 4, core: 2. Of those that a mesh axis runs over, the one named last changes fastest.
Arguments:
- tokens: bfloat16 [32, 1024, 1536], P(('shard', 'rep')), may hold values from -6 to 6
- norm_gain: bfloat16 [1536], P('shard'), may hold values from 0.5 to 1.5
- in_weight: bfloat16 [1536, 6448], P('shard'), may hold values from -0.15625 to 0.15625
- conv_weight: bfloat16 [4, 3328], P(None, 'shard'), may hold values from -0.5 to 0.5
- conv_bias: bfloat16 [3328], P('shard'), may hold values from -0.5 to 0.5
- dt_bias: bfloat16 [48], P('shard'), may hold values from -4 to -1
- a_log: bfloat16 [48], P('shard'), may hold values from -4 to 1.5
- skip: bfloat16 [48], P('shard'), may hold values from 0.5 to 1.5
- gate_gain: bfloat16 [3072], P('shard'), may hold values from 0.5 to 1.5
- out_weight: bfloat16 [3072, 1536], P('shard'), may hold values from -0.109375 to 0.109375
- cotangent: bfloat16 [32, 1024, 1536], P(('shard', 'rep')), may hold values from -6 to 6
Outputs:
- output: bfloat16 [32, 1024, 1536], P(('shard', 'rep'))
- input_grad: float32 [32, 1024, 1536], P(('shard', 'rep'))
- norm_gain_grad: float32 [1536], P('shard')
- in_weight_grad: float32 [1536, 6448], P('shard')
- conv_weight_grad: float32 [4, 3328], P(None, 'shard')
- conv_bias_grad: float32 [3328], P('shard')
- dt_bias_grad: float32 [48], P('shard')
- a_log_grad: float32 [48], P('shard')
- skip_grad: float32 [48], P('shard')
- gate_gain_grad: float32 [3072], P('shard')
- out_weight_grad: float32 [3072, 1536], P('shard')
All inputs are finite; a program needn't handle non-finite values.
Results may differ from a plain program's by a relative error of at most 0.0077.
Values may be sent and summed in bfloat16 or wider, within the bound.
No kernel may reach another device: no remote copies, remote signals or barrier semaphores. Data moves between devices by JAX's collectives and lax.ppermute only.
A program may use at most 448 MiB of HBM per device.

v0:
```python
import jax
import jax.numpy as jnp
from jax import lax
from jax.sharding import PartitionSpec as P

STRETCH = 256
epsilon = 1e-05


def rms_scale(values, gain):
    return values * lax.rsqrt(jnp.mean(values * values, axis=-1, keepdims=True) + epsilon) * gain


def stretch_step(state, values, keys_b, keys_c, steps, decay_rate):
    logs = jnp.cumsum(steps * decay_rate, axis=0)
    span = logs.shape[0]
    rows = lax.broadcasted_iota(jnp.int32, (span, span), 0)
    cols = lax.broadcasted_iota(jnp.int32, (span, span), 1)
    causal = (rows >= cols)[None, :, :]
    logs_heads = logs.T
    gaps = logs_heads[:, :, None] - logs_heads[:, None, :]
    weights = jnp.where(causal, jnp.exp(jnp.where(causal, gaps, 0.0)), 0.0)
    inner = jnp.dot(keys_c, keys_b.T, precision=lax.Precision.HIGHEST)
    mixing = inner[None, :, :] * weights * steps.T[:, None, :]
    local = jnp.einsum("hts,shp->thp", mixing, values, precision=lax.Precision.HIGHEST)
    carried = (
        jnp.einsum("hpn,tn->thp", state, keys_c, precision=lax.Precision.HIGHEST)
        * jnp.exp(logs)[:, :, None]
    )
    last = logs[-1]
    tails = jnp.exp(last[None, :] - logs) * steps
    scaled = values * tails[:, :, None]
    fresh = jnp.einsum("shp,sn->hpn", scaled, keys_b, precision=lax.Precision.HIGHEST)
    new_state = jnp.exp(last)[:, None, None] * state + fresh
    return (new_state, (local + carried).reshape(span, -1))


def mixer(proj, conv_weight, conv_bias, dt_bias, a_log, skip, gate_gain):
    length = proj.shape[0]
    inner_width = gate_gain.shape[0]
    state_size = (conv_bias.shape[0] - inner_width) // 2
    heads = dt_bias.shape[0]
    head_width = inner_width // heads
    taps = conv_weight.shape[0]
    gate = proj[:, :inner_width]
    conv_in = proj[:, inner_width : 2 * inner_width + 2 * state_size]
    raw_steps = proj[:, 2 * inner_width + 2 * state_size :]
    padded = jnp.pad(conv_in, ((taps - 1, 0), (0, 0)))
    conv_sum = jnp.zeros_like(conv_in) + conv_bias
    for offset in range(taps):
        conv_sum = conv_sum + conv_weight[offset] * padded[offset : offset + length]
    act = jax.nn.silu(conv_sum)
    values = act[:, :inner_width]
    keys_b = act[:, inner_width : inner_width + state_size]
    keys_c = act[:, inner_width + state_size :]
    steps = jax.nn.softplus(raw_steps + dt_bias)
    decay_rate = -jnp.exp(a_log)
    blocks = length // STRETCH

    def advance(state, block_values, block_b, block_c, block_steps):
        return stretch_step(
            state,
            block_values.reshape(STRETCH, heads, head_width),
            block_b,
            block_c,
            block_steps,
            decay_rate,
        )

    stepper = jax.checkpoint(advance)
    state = jnp.zeros((heads, head_width, state_size), jnp.float32)
    outputs = []
    for index in range(blocks):
        lower = index * STRETCH
        state, piece = stepper(
            state,
            values[lower : lower + STRETCH],
            keys_b[lower : lower + STRETCH],
            keys_c[lower : lower + STRETCH],
            steps[lower : lower + STRETCH],
        )
        outputs.append(piece)
    scan_flat = jnp.concatenate(outputs, axis=0)
    skip_cols = jnp.repeat(skip, head_width)
    scan_out = scan_flat + skip_cols[None, :] * values
    gated = scan_out * jax.nn.silu(gate)
    return rms_scale(gated, gate_gain)


def on_device(
    tokens,
    norm_gain,
    in_weight,
    conv_weight,
    conv_bias,
    dt_bias,
    a_log,
    skip,
    gate_gain,
    out_weight,
    cotangent,
):
    whole = (
        lax.all_gather(norm_gain, "shard", axis=0, tiled=True),
        lax.all_gather(in_weight, "shard", axis=0, tiled=True),
        lax.all_gather(conv_weight, "shard", axis=1, tiled=True),
        lax.all_gather(conv_bias, "shard", axis=0, tiled=True),
        lax.all_gather(dt_bias, "shard", axis=0, tiled=True),
        lax.all_gather(a_log, "shard", axis=0, tiled=True),
        lax.all_gather(skip, "shard", axis=0, tiled=True),
        lax.all_gather(gate_gain, "shard", axis=0, tiled=True),
        lax.all_gather(out_weight, "shard", axis=0, tiled=True),
    )
    (
        gain_full,
        in_full,
        conv_w_full,
        conv_b_full,
        dt_full,
        alog_full,
        skip_full,
        gate_full,
        out_full,
    ) = whole
    small = tuple(
        (
            item.astype(jnp.float32)
            for item in (conv_w_full, conv_b_full, dt_full, alog_full, skip_full, gate_full)
        )
    )
    seqs, length, width = tokens.shape
    total_rows = seqs * length
    flat = tokens.reshape(total_rows, width).astype(jnp.float32)
    normed_f, norm_pull = jax.vjp(rms_scale, flat, gain_full.astype(jnp.float32))
    normed = normed_f.astype(jnp.bfloat16)
    proj = jnp.dot(normed, in_full, preferred_element_type=jnp.float32)

    def mix_all(proj_rows, conv_w, conv_b, dt_b, alog_v, skip_v, gate_g):
        shaped = proj_rows.reshape(seqs, length, proj_rows.shape[1])
        mixed_rows = jax.vmap(mixer, in_axes=(0, None, None, None, None, None, None))(
            shaped, conv_w, conv_b, dt_b, alog_v, skip_v, gate_g
        )
        return mixed_rows.reshape(total_rows, mixed_rows.shape[2])

    mixed_f, mix_pull = jax.vjp(mix_all, proj, *small)
    mixed = mixed_f.astype(jnp.bfloat16)
    branch_out = jnp.dot(mixed, out_full, preferred_element_type=jnp.float32)
    output = (flat + branch_out).astype(jnp.bfloat16).reshape(seqs, length, width)
    in_back, out_back = (
        lax.all_gather(in_weight, "shard", axis=0, tiled=True),
        lax.all_gather(out_weight, "shard", axis=0, tiled=True),
    )
    cot_rows = cotangent.reshape(total_rows, width)
    mixed_grad = lax.dot_general(
        cot_rows, out_back, (((1,), (1,)), ((), ())), preferred_element_type=jnp.float32
    )
    mix_grads = mix_pull(mixed_grad)
    proj_grad = mix_grads[0].astype(jnp.bfloat16)
    normed_grad = lax.dot_general(
        proj_grad, in_back, (((1,), (1,)), ((), ())), preferred_element_type=jnp.float32
    )
    flat_grad, gain_grad = norm_pull(normed_grad)
    input_grad = (cot_rows.astype(jnp.float32) + flat_grad).reshape(seqs, length, width)
    out_grad = lax.dot_general(
        mixed, cot_rows, (((0,), (0,)), ((), ())), preferred_element_type=jnp.float32
    )
    in_grad = lax.dot_general(
        normed, proj_grad, (((0,), (0,)), ((), ())), preferred_element_type=jnp.float32
    )
    owned = (
        lax.psum_scatter(gain_grad, "shard", scatter_dimension=0, tiled=True),
        lax.psum_scatter(in_grad, "shard", scatter_dimension=0, tiled=True),
        lax.psum_scatter(mix_grads[1], "shard", scatter_dimension=1, tiled=True),
        lax.psum_scatter(mix_grads[2], "shard", scatter_dimension=0, tiled=True),
        lax.psum_scatter(mix_grads[3], "shard", scatter_dimension=0, tiled=True),
        lax.psum_scatter(mix_grads[4], "shard", scatter_dimension=0, tiled=True),
        lax.psum_scatter(mix_grads[5], "shard", scatter_dimension=0, tiled=True),
        lax.psum_scatter(mix_grads[6], "shard", scatter_dimension=0, tiled=True),
        lax.psum_scatter(out_grad, "shard", scatter_dimension=0, tiled=True),
    )
    summed = lax.psum(
        (owned[0], owned[1], owned[2], owned[3], owned[4], owned[5], owned[6], owned[7], owned[8]),
        "rep",
    )
    return (
        output,
        input_grad,
        summed[0],
        summed[1],
        summed[2],
        summed[3],
        summed[4],
        summed[5],
        summed[6],
        summed[7],
        summed[8],
    )


def solution(mesh):
    placed = (
        P(("shard", "rep"), None, None),
        P("shard"),
        P("shard", None),
        P(None, "shard"),
        P("shard"),
        P("shard"),
        P("shard"),
        P("shard"),
        P("shard"),
        P("shard", None),
        P(("shard", "rep"), None, None),
    )
    return jax.shard_map(
        on_device,
        mesh=mesh,
        in_specs=placed,
        out_specs=(
            P(("shard", "rep"), None, None),
            P(("shard", "rep"), None, None),
            P("shard"),
            P("shard", None),
            P(None, "shard"),
            P("shard"),
            P("shard"),
            P("shard"),
            P("shard"),
            P("shard"),
            P("shard", None),
        ),
        check_vma=False,
    )
```

profile of v0, /device:TPU:0, one launch (start us, length us, event | category | flops | bytes accessed | tf_op | source)
XLA Modules:
  0.0 1886.3 jit_solution(5279300305673587679)
XLA Ops:
  43.6 94.0 %all-gather.6.cloned.1.call-done = bf16[1536,6448]{0,1:T(8,128)(2,1)} async-done(((bf16[384,6448]{0,1:T(8,128)(2,1)}), bf16[1536,6448]{0,1:T(8,128)(2,1)}) %all-gather.6.cloned.1.call-update) | async-done | bytes 19808272 | tf_op jit(solution)/shard_map/all_gather | solution.py:105
  137.6 29.2 %convolution_bitcast_fusion = f32[1,1024,6448]{2,1,0:T(8,128)} fusion(bf16[1536,6448]{0,1:T(8,128)(2,1)} %all-gather.6.cloned.1.call-done, bf16[1,1024,1536]{2,1,0:T(8,128)(2,1)S(1)} %copy-done.29, f32[1536]{0:T(1024)S(1)} %reshape.1986, f32[1024]{0:T(1024)S(1)} %fusion.294), kind=kOutput, calls=%fused_computation.4 | convolution fusion | flops 20289945600 | bytes 49375232 | tf_op jit(solution)/shard_map/dot_general | solution.py:136
  200.2 24.7 %fusion.2 = (f32[1,1024,3328]{2,1,0:T(8,128)S(1)}, f32[1,1024,3328]{2,1,0:T(8,128)}) fusion(f32[1,1024,3328]{2,1,0:T(8,128)} %slice.245, f32[3328]{0:T(1024)} %get-tuple-element.111, f32[3328]{0:T(1024)} %get-tuple-element.112, f32[3328]{0:T(1024)} %get-tuple-element.113, f32[3328]{0:T(1024)} %get-tuple-element.110, f32[3328]{0:T(1024)} %convert_element_type.62), kind=kLoop, calls=%fused_computation.15 | loop fusion | flops 40894464 | bytes 40961024 | tf_op jit(solution)/shard_map/jvp(vmap(jit(silu)))/mul | solution.py:52
  231.6 15.2 fusion.336
  279.6 17.2 bitcast_add_fusion.6
  324.3 16.2 bitcast_add_fusion.3
  352.6 17.0 bitcast_add_fusion.4
  381.9 17.1 bitcast_add_fusion.5
  402.5 18.6 multiply_reduce_fusion.13
  423.4 17.6 fusion.139
  441.0 19.8 %fusion.6 = (f32[3072]{0:T(1024)}, f32[1024]{0:T(1024)S(1)}, f32[1024,3072]{1,0:T(8,128)}) fusion(f32[1,1024,3072]{2,1,0:T(8,128)} %get-tuple-element.145, f32[1024]{0:T(1024)S(1)} %fusion.295, f32[3072]{0:T(1024)S(1)} %bitcast.1060, bf16[3072,1536]{1,0:T(8,128)(2,1)} %all-gather.8.cloned.1.call-done, bf16[1,1024,1536]{2,1,0:T(8,128)(2,1)} %param.21), kind=kOutput, calls=%fused_computation.24 | convolution fusion | flops 9682546688 | bytes 37781504 | tf_op jit(solution)/shard_map/dot_general | solution.py:154
  460.8 32.0 %multiply_reduce_fusion.4 = (f32[3072]{0:T(1024)}, f32[1,1024,3072]{2,1,0:T(8,128)}, f32[1,1024,3072]{2,1,0:T(8,128)}) fusion(f32[1,1024,3328]{2,1,0:T(8,128)} %copy-done, f32[1,1024,6448]{2,1,0:T(8,128)} %convolution_bitcast_fusion, f32[1,1024,3072]{2,1,0:T(8,128)} %get-tuple-element.145, f32[1024]{0:T(1024)S(1)} %multiply_multiply_fusion.1, ...), kind=kLoop, calls=%fused_computation.27 | loop fusion | flops 75494400 | bytes 88125440 | tf_op jit(solution)/shard_map/transpose(jvp(vmap()))/reduce_sum | solution.py:85
  734.4 46.2 %fusion.65 = (f32[48,256]{1,0:T(8,128)S(1)}, f32[48,256]{1,0:T(8,128)S(1)}, f32[48,256]{1,0:T(8,128)}, f32[256,256]{1,0:T(8,128)}, f32[256,256]{1,0:T(8,128)}, /...) fusion(f32[48,256]{1,0:T(8,128)S(1)} %copy-done.105, ...), kind=kOutput, calls=%fused_computation.108 | convolution fusion | flops 2604253184 | bytes 47185920 | tf_op jit(solution)/shard_map/transpose(jvp(vmap(jvp(vmap()))))/checkpoint/hts,shp->thp/dot_general | solution.py:25
  801.5 14.1 bitcast_add_fusion.2
  835.1 14.0 bitcast_add_fusion.1
  1002.8 36.0 %multiply_reduce_fusion.2 = (f32[3328]{0:T(1024)S(1)}, f32[3328]{0:T(1024)S(1)}, f32[3328]{0:T(1024)S(1)}, f32[3328]{0:T(1024)}, f32[3328]{0:T(1024)S(1)}, /*index=5*/f32[1,1024,3328]{2,1,0:T(8,128)}) fusion(f32[1,1024,3328]{2,1,0:T(8,128)} %slice.245, f32[1,1024,6448]{2,1,0:T(8,128)} %convolution_bitcast_fusion, f32[1,1024,3328]{2,1,0:T(8,128)} %get-tuple-element.153, ...), kind=kLoop, calls=%fused_computation.12 | loop fusion | flops 68140800 | bytes 68224000 | tf_op jit(solution)/shard_map/transpose(jvp(vmap()))/reduce_sum | solution.py:51
  1038.8 17.1 broadcast_multiply_fusion
  1055.9 19.7 %pad_add_fusion = f32[1,1024,3328]{2,1,0:T(8,128)} fusion(f32[1,1024,3328]{2,1,0:T(8,128)} %get-tuple-element.156, f32[1,1024,3328]{2,1,0:T(8,128)} %get-tuple-element.157, f32[1,1024,3328]{2,1,0:T(8,128)} %get-tuple-element.158, f32[1,1024,3328]{2,1,0:T(8,128)S(1)} %get-tuple-element.155), kind=kLoop, calls=%fused_computation.7 | loop fusion | flops 10223616 | bytes 68157440 | tf_op jit(solution)/shard_map/transpose(jvp(vmap()))/add_any | solution.py:51
  1075.6 33.5 %fusion.133 = f32[1536,6448]{0,1:T(8,128)} fusion(bf16[1,1024,1536]{2,1,0:T(8,128)(2,1)S(1)} %copy-done.30, f32[1536]{0:T(1024)S(1)} %copy-done.125, f32[1024]{0:T(1024)S(1)} %copy-done.129, f32[1,1024,3072]{2,1,0:T(8,128)} %get-tuple-element.154, f32[1,1024,3328]{2,1,0:T(8,128)} %pad_add_fusion, f32[1,1024,48]{2,1,0:T(8,128)} %get-tuple-element.136), kind=kOutput, calls=%fused_computation.176 | convolution fusion | flops 20309753856 | bytes 69183488 | tf_op jit(solution)/shard_map/dot_general | solution.py:167
  1111.1 267.0 %reduce-scatter.6.cloned.1.call-done = f32[384,6448]{0,1:T(8,128)} async-done(((f32[1536,6448]{0,1:T(8,128)}), f32[384,6448]{0,1:T(8,128)}) %reduce-scatter.6.cloned.1.call-update) | async-done | bytes 9904144 | tf_op jit(solution)/shard_map/reduce_scatter | solution.py:172
  1381.0 33.0 %fusion.73 = (f32[1536]{0:T(1024)S(1)}, f32[1024]{0:T(1024)S(1)}, f32[1024,1536]{1,0:T(8,128)}) fusion(bf16[1,1024,1536]{2,1,0:T(8,128)(2,1)S(1)} %copy-done.30, f32[1024]{0:T(1024)S(1)} %copy-done.129, f32[1536]{0:T(1024)S(1)} %copy-done.125, bf16[1536,6448]{0,1:T(8,128)(2,1)} %all-gather.6.cloned.1.call-done, f32[1,1024,3072]{2,1,0:T(8,128)} %get-tuple-element.154, ...), kind=kOutput, calls=%fused_computation.116 | convolution fusion | flops 20314468352 | bytes 55676928 | tf_op jit(solution)/shard_map/dot_general | solution.py:159
  1432.0 17.0 fusion.131
  1450.2 40.2 %all-reduce.44 = (f32[384]{0:T(512)}, f32[4,832]{1,0:T(4,128)}, f32[832]{0:T(1024)}, f32[12]{0:T(128)}, f32[12]{0:T(128)}, /*index=5*/f32[12]{0:T(128)}, f32[768]{0:T(1024)}) all-reduce(f32[384]{0:T(512)S(1)} %dynamic-slice.5, f32[4,832]{1,0:T(4,128)S(1)} %copy.695, ...), channel_id=1, replica_groups=mesh['shard'=4,'rep'=8] {'rep'}, use_global_device_ids=true, to_apply=%region_59.60 | all-reduce | flops 5348 | bytes 42784 | tf_op jit(solution)/shard_map/psum | solution.py:181
  1490.4 378.2 %all-reduce.50.cloned.1.call-done = (f32[384,6448]{0,1:T(8,128)}, f32[768,1536]{1,0:T(8,128)}) async-done(((f32[384,6448]{0,1:T(8,128)}, f32[768,1536]{1,0:T(8,128)}), (f32[384,6448]{0,1:T(8,128)}, f32[768,1536]{1,0:T(8,128)})) %all-reduce.50.cloned.1.call-update) | async-done | bytes 14622736 | tf_op jit(solution)/shard_map/psum | solution.py:181
  (655 shorter events, 631.4 us)
Async XLA Ops:
  7.2 130.3 %all-gather.6.cloned.1.call-start = ((), (), s32[]{:S(2)}) async-start(), calls=%async_computation.3 | async-start | bytes 24760320 | tf_op jit(solution)/shard_map/all_gather | solution.py:105
  8.0 433.0 %all-gather.8.cloned.1.call-start = ((), (), s32[]{:S(2)}) async-start(), calls=%async_computation.4 | async-start | bytes 11796480 | tf_op jit(solution)/shard_map/all_gather | solution.py:112
  8.7 1102.4 %reduce-scatter.8.cloned.1.call-start = ((), (), s32[]{:S(2)}) async-start(), calls=%async_computation.6 | async-start | bytes 23592960 | tf_op jit(solution)/shard_map/reduce_scatter | solution.py:179
  14.7 152.1 %copy-start.128 = (f32[1024]{0:T(1024)}, f32[1024]{0:T(1024)S(1)}, u32[]{:S(2)}) copy-start(f32[1024]{0:T(1024)S(1)} %fusion.294) | copy-start | bytes 12292
  20.9 145.9 %copy-start.124 = (f32[1536]{0:T(1024)}, f32[1536]{0:T(1024)S(1)}, u32[]{:S(2)}) copy-start(f32[1536]{0:T(1024)S(1)} %reshape.1986) | copy-start | bytes 18436
  29.9 138.2 %copy-start.119 = (f32[48]{0:T(128)}, f32[48]{0:T(128)S(1)}, u32[]{:S(2)}) copy-start(f32[48]{0:T(128)S(1)} %fusion.296) | copy-start | bytes 580
  29.9 136.9 %copy-start.134 = (f32[48]{0:T(128)}, f32[48]{0:T(128)S(1)}, u32[]{:S(2)}) copy-start(f32[48]{0:T(128)S(1)} %convert_element_type.66) | copy-start | bytes 580
  310.6 320.8 %copy-start.1 = (f32[48,64,128]{2,1,0:T(8,128)}, f32[48,64,128]{2,1,0:T(8,128)S(1)}, u32[]{:S(2)}) copy-start(f32[48,64,128]{2,1,0:T(8,128)S(1)} %convolution_add_fusion) | copy-start | bytes 4718596
  315.7 296.4 %copy-start.3 = (f32[48,64,128]{2,1,0:T(8,128)}, f32[48,64,128]{2,1,0:T(8,128)S(1)}, u32[]{:S(2)}) copy-start(f32[48,64,128]{2,1,0:T(8,128)S(1)} %multiply_add_fusion.2) | copy-start | bytes 4718596
  423.4 100.8 %copy-start.44 = (f32[1,256,128]{2,1,0:T(8,128)}, f32[1,256,128]{2,1,0:T(8,128)S(1)}, u32[]{:S(2)}) copy-start(f32[1,256,128]{2,1,0:T(8,128)S(1)} %get-tuple-element.42) | copy-start | bytes 393220
  423.4 131.6 %copy-start.41 = (f32[1,256,128]{2,1,0:T(8,128)}, f32[1,256,128]{2,1,0:T(8,128)S(1)}, u32[]{:S(2)}) copy-start(f32[1,256,128]{2,1,0:T(8,128)S(1)} %get-tuple-element.54) | copy-start | bytes 393220
  601.1 777.1 %reduce-scatter.6.cloned.1.call-start = ((), (), s32[]{:S(2)}) async-start(), calls=%async_computation.5 | async-start | bytes 49520640 | tf_op jit(solution)/shard_map/reduce_scatter | solution.py:172
  734.4 46.3 %copy-start.20 = (f32[48,64,128]{2,1,0:T(8,128)S(1)}, f32[48,64,128]{2,1,0:T(8,128)}, u32[]{:S(2)}) copy-start(f32[48,64,128]{2,1,0:T(8,128)} %copy-done.19) | copy-start | bytes 4718596
  734.4 46.3 %copy-start.45 = (f32[1,256,128]{2,1,0:T(8,128)S(1)}, f32[1,256,128]{2,1,0:T(8,128)}, u32[]{:S(2)}) copy-start(f32[1,256,128]{2,1,0:T(8,128)} %copy-done.44) | copy-start | bytes 393220
  734.4 49.0 %copy-start.71 = (f32[1,256,48]{1,0,2:T(1,128)S(1)}, f32[1,256,48]{1,0,2:T(1,128)}, u32[]{:S(2)}) copy-start(f32[1,256,48]{1,0,2:T(1,128)} %copy-done.70) | copy-start | bytes 147460
  734.4 59.7 %copy-start.51 = (f32[1,48,256]{1,2,0:T(8,128)S(1)}, f32[1,48,256]{1,2,0:T(8,128)}, u32[]{:S(2)}) copy-start(f32[1,48,256]{1,2,0:T(8,128)} %copy-done.50) | copy-start | bytes 147460
  734.4 59.7 %copy-start.37 = (f32[1,256,48]{2,1,0:T(8,128)S(1)}, f32[1,256,48]{2,1,0:T(8,128)}, u32[]{:S(2)}) copy-start(f32[1,256,48]{2,1,0:T(8,128)} %get-tuple-element.49) | copy-start | bytes 147460
  734.4 60.7 %copy-start.4 = (f32[48,64,128]{2,1,0:T(8,128)S(1)}, f32[48,64,128]{2,1,0:T(8,128)}, u32[]{:S(2)}) copy-start(f32[48,64,128]{2,1,0:T(8,128)} %copy-done.3) | copy-start | bytes 4718596
  1109.1 271.7 %copy-start.118 = (f32[3072]{0:T(1024)S(1)}, f32[3072]{0:T(1024)}, u32[]{:S(2)}) copy-start(f32[3072]{0:T(1024)} %get-tuple-element.133) | copy-start | bytes 36868
  1109.1 271.9 %copy-start.138 = (f32[48]{0:T(128)S(1)}, f32[48]{0:T(128)}, u32[]{:S(2)}) copy-start(f32[48]{0:T(128)} %get-tuple-element.201) | copy-start | bytes 580
  1109.1 271.9 %copy-start.139 = (f32[48]{0:T(128)S(1)}, f32[48]{0:T(128)}, u32[]{:S(2)}) copy-start(f32[48]{0:T(128)} %get-tuple-element.199) | copy-start | bytes 580
  1109.1 271.9 %copy-start.141 = (bf16[48]{0:T(256)(128)(2,1)S(1)}, bf16[48]{0:T(256)(128)(2,1)}, u32[]{:S(2)}) copy-start(bf16[48]{0:T(256)(128)(2,1)} %copy-done.140) | copy-start | bytes 292
  1109.1 340.0 %reduce-scatter.10.cloned.1.call-start = ((), (), s32[]{:S(2)}) async-start(), calls=%async_computation.7 | async-start | bytes 2129920
  1111.0 757.6 %all-reduce.50.cloned.1.call-start = ((), (), s32[]{:S(2)}) async-start(), calls=%async_computation.8 | async-start | bytes 29245440 | tf_op jit(solution)/shard_map/psum | solution.py:181
  (130 other events, 2236.2 us)
Sparse Core Ops, SparseCore 0:
  9.6 127.9 all-gather.5
  139.1 64.2 all-gather.7
  601.2 137.8 reduce-scatter.7
  1109.2 268.9 reduce-scatter.5
  1381.1 28.7 reduce-scatter.9
  1414.1 454.4 all-reduce.49
where the time goes:
time: 1890 us
  waiting for transfers between devices  741 us (39%)
  matrix products  494 us (26%)
  local copies, waits for them, and re-layouts  285 us (15%)
  other arithmetic  270 us (14%)
  blocking collectives  76.3 us (4%)
  between operations  20.3 us (1%)
    psum x1, waiting for transfers between devices, on_device(): lax.psum((owned[0], owned[1], owned[2], owned[3], owned[4], owned[5], own...  378 us
    reduce_scatter x1, waiting for transfers between devices, on_device(): lax.psum_scatter(in_grad, 'shard', scatter_dimension=0, tiled=True)  267 us
    dot_general x12, matrix products, stretch_step(): jnp.einsum('hts,shp->thp', mixing, values, precision=lax.Precision.HIGHEST)  210 us
    all_gather x1, waiting for transfers between devices, on_device(): lax.all_gather(in_weight, 'shard', axis=0, tiled=True)  94 us
    dot_general x15, matrix products, stretch_step(): jnp.einsum('hpn,tn->thp', state, keys_c, precision=lax.Precision.HIGHEST)  72.1 us
    mul x24, local copies, waits for them, and re-layouts, stretch_step(): scaled = values * tails[:, :, None]  56.4 us
    dot_general x9, matrix products, stretch_step(): jnp.einsum('shp,sn->hpn', scaled, keys_b, precision=lax.Precision.HIGHEST)  48.5 us
    psum x1, blocking collectives, on_device(): lax.psum((owned[0], owned[1], owned[2], owned[3], owned[4], owned[5], own...  40.2 us
  transfers between devices with their start and end apart: 6, of which 3 were waited for; matrix products, arithmetic and copies ran while one was open for 46% of the time, Pallas kernels for 0%

commit v1 on v0

--- a/solution.py
+++ b/solution.py
@@ -5,6 +5,22 @@
 
 STRETCH = 256
 epsilon = 1e-05
+
+
+def collect(x, axis, dim):
+    ways, here, step = (lax.axis_size(axis), lax.axis_index(axis), x.shape[dim])
+    shape = [n * ways if d == dim else n for d, n in enumerate(x.shape)]
+    full = lax.dynamic_update_slice_in_dim(jnp.zeros(shape, x.dtype), x, here * step, axis=dim)
+    going_up = going_down = x
+    for far in range(1, ways // 2 + 1):
+        going_up = lax.ppermute(going_up, axis, [(d, (d + 1) % ways) for d in range(ways)])
+        full = lax.dynamic_update_slice_in_dim(full, going_up, (here - far) % ways * step, axis=dim)
+        if 2 * far < ways:
+            going_down = lax.ppermute(going_down, axis, [(d, (d - 1) % ways) for d in range(ways)])
+            full = lax.dynamic_update_slice_in_dim(
+                full, going_down, (here + far) % ways * step, axis=dim
+            )
+    return full
 
 
 def rms_scale(values, gain):
@@ -102,7 +118,7 @@
 ):
     whole = (
         lax.all_gather(norm_gain, "shard", axis=0, tiled=True),
-        lax.all_gather(in_weight, "shard", axis=0, tiled=True),
+        collect(in_weight, "shard", 0),
         lax.all_gather(conv_weight, "shard", axis=1, tiled=True),
         lax.all_gather(conv_bias, "shard", axis=0, tiled=True),
         lax.all_gather(dt_bias, "shard", axis=0, tiled=True),

time: 1890 us -> 2160 us (1.14)
  waiting for transfers between devices: 741 us -> 877 us
  blocking collectives: 76.3 us -> 174 us
  local copies, waits for them, and re-layouts: 285 us -> 313 us
    ppermute x0 -> x3, waiting for transfers between devices: none -> 105 us  [the longest x2 105 us: collect(): lax.ppermute(going_up, axis, [(d, (d + 1) % ways) for d in range(ways)])]
    all_gather x1, blocking collectives: 6.14 us -> 101 us  [on_device(): lax.all_gather(norm_gain, 'shard', axis=0, tiled=True)]
    all_gather x1, waiting for transfers between devices: 94 us -> 125 us  [on_device(): lax.all_gather(in_weight, 'shard', axis=0, tiled=True)]
  transfers between devices with their start and end apart: 6 -> 9, of which waited for: 3 -> 5; matrix products, arithmetic and copies ran while one was open for 46% -> 49% of each run, Pallas kernels for 0% -> 0%
where the time goes in v1:
time: 2160 us
  waiting for transfers between devices  877 us (41%)
  matrix products  494 us (23%)
  local copies, waits for them, and re-layouts  313 us (14%)
  other arithmetic  274 us (13%)
  blocking collectives  174 us (8%)
    psum x1, waiting for transfers between devices, on_device(): lax.psum((owned[0], owned[1], owned[2], owned[3], owned[4], owned[5], own...  368 us
    reduce_scatter x1, waiting for transfers between devices, on_device(): lax.psum_scatter(in_grad, 'shard', scatter_dimension=0, tiled=True)  266 us
    dot_general x12, matrix products, stretch_step(): jnp.einsum('hts,shp->thp', mixing, values, precision=lax.Precision.HIGHEST)  210 us
    all_gather x1, waiting for transfers between devices, on_device(): lax.all_gather(in_weight, 'shard', axis=0, tiled=True)  125 us
    ppermute x2, waiting for transfers between devices, collect(): lax.ppermute(going_up, axis, [(d, (d + 1) % ways) for d in range(ways)])  105 us
    all_gather x1, blocking collectives, on_device(): lax.all_gather(norm_gain, 'shard', axis=0, tiled=True)  101 us
    dot_general x15, matrix products, stretch_step(): jnp.einsum('hpn,tn->thp', state, keys_c, precision=lax.Precision.HIGHEST)  71.3 us
    mul x24, local copies, waits for them, and re-layouts, stretch_step(): scaled = values * tails[:, :, None]  56.3 us
  transfers between devices with their start and end apart: 9, of which 5 were waited for; matrix products, arithmetic and copies ran while one was open for 49% of the time, Pallas kernels for 0%

profile of v1, /device:TPU:0, one launch (start us, length us, event | category | flops | bytes accessed | tf_op | source)
XLA Modules:
  0.0 2157.4 jit_solution(5344817318151527429)
XLA Ops:
  9.7 105.0 %collective-permute-done = bf16[384,6448]{0,1:T(8,128)(2,1)} collective-permute-done((bf16[384,6448]{0,1:T(8,128)(2,1)}, bf16[384,6448]{0,1:T(8,128)(2,1)}, u32[]{:S(2)}, u32[]{:S(2)}) %collective-permute-start) | collective-permute-done | bytes 4952096 | tf_op jit(solution)/shard_map/ppermute | solution.py:16
  121.3 101.2 %all-gather.1 = bf16[4,1,384]{2,1,0:T(2,128)(2,1)S(1)} all-gather(bf16[1,1,384]{2,1,0:T(2,128)(2,1)S(1)} %reshape.1982), channel_id=1, replica_groups=mesh['shard'=4,'rep'=8] {'shard'}, dimensions={0}, use_global_device_ids=true | all-gather | bytes 3840 | tf_op jit(solution)/shard_map/all_gather | solution.py:120
  280.0 29.2 %convolution_bitcast_fusion = f32[1,1024,6448]{2,1,0:T(8,128)} fusion(bf16[1536,6448]{0,1:T(8,128)(2,1)} %constant_dynamic-update-slice_fusion, bf16[1,1024,1536]{2,1,0:T(8,128)(2,1)S(1)} %copy-done.29, f32[1536]{0:T(1024)S(1)} %reshape.1986, f32[1024]{0:T(1024)S(1)} %fusion.294), kind=kOutput, calls=%fused_computation.4 | convolution fusion | flops 20289945600 | bytes 49375232 | tf_op jit(solution)/shard_map/dot_general | solution.py:152
  342.5 25.1 %fusion.2 = (f32[1,1024,3328]{2,1,0:T(8,128)S(1)}, f32[1,1024,3328]{2,1,0:T(8,128)}) fusion(f32[1,1024,3328]{2,1,0:T(8,128)} %slice.245, f32[3328]{0:T(1024)} %get-tuple-element.111, f32[3328]{0:T(1024)} %get-tuple-element.112, f32[3328]{0:T(1024)} %get-tuple-element.113, f32[3328]{0:T(1024)} %get-tuple-element.110, f32[3328]{0:T(1024)} %convert_element_type.62), kind=kLoop, calls=%fused_computation.15 | loop fusion | flops 40894464 | bytes 40961024 | tf_op jit(solution)/shard_map/jvp(vmap(jit(silu)))/mul | solution.py:68
  374.3 15.0 fusion.336
  422.1 17.2 bitcast_add_fusion.6
  466.6 16.4 bitcast_add_fusion.3
  495.1 17.0 bitcast_add_fusion.4
  524.3 17.1 bitcast_add_fusion.5
  544.9 18.6 multiply_reduce_fusion.13
  565.8 17.3 fusion.139
  583.2 22.4 %fusion.6 = (f32[3072]{0:T(1024)}, f32[1024]{0:T(1024)S(1)}, f32[1024,3072]{1,0:T(8,128)}) fusion(f32[1,1024,3072]{2,1,0:T(8,128)} %get-tuple-element.145, f32[1024]{0:T(1024)S(1)} %fusion.295, f32[3072]{0:T(1024)S(1)} %bitcast.1062, bf16[3072,1536]{1,0:T(8,128)(2,1)} %all-gather.6.cloned.1.call-done, bf16[1,1024,1536]{2,1,0:T(8,128)(2,1)} %param.21), kind=kOutput, calls=%fused_computation.24 | convolution fusion | flops 9682546688 | bytes 37781504 | tf_op jit(solution)/shard_map/dot_general | solution.py:170
  605.6 33.0 %multiply_reduce_fusion.4 = (f32[3072]{0:T(1024)}, f32[1,1024,3072]{2,1,0:T(8,128)}, f32[1,1024,3072]{2,1,0:T(8,128)}) fusion(f32[1,1024,3328]{2,1,0:T(8,128)} %copy-done, f32[1,1024,6448]{2,1,0:T(8,128)} %convolution_bitcast_fusion, f32[1,1024,3072]{2,1,0:T(8,128)} %get-tuple-element.145, f32[1024]{0:T(1024)S(1)} %multiply_multiply_fusion.1, ...), kind=kLoop, calls=%fused_computation.27 | loop fusion | flops 75494400 | bytes 88125440 | tf_op jit(solution)/shard_map/transpose(jvp(vmap()))/reduce_sum | solution.py:101
  879.0 46.2 %fusion.65 = (f32[48,256]{1,0:T(8,128)S(1)}, f32[48,256]{1,0:T(8,128)S(1)}, f32[48,256]{1,0:T(8,128)}, f32[256,256]{1,0:T(8,128)}, f32[256,256]{1,0:T(8,128)}, /...) fusion(f32[48,256]{1,0:T(8,128)S(1)} %copy-done.105, ...), kind=kOutput, calls=%fused_computation.108 | convolution fusion | flops 2604253184 | bytes 47185920 | tf_op jit(solution)/shard_map/transpose(jvp(vmap(jvp(vmap()))))/checkpoint/hts,shp->thp/dot_general | solution.py:41
  1147.5 36.1 %multiply_reduce_fusion.2 = (f32[3328]{0:T(1024)S(1)}, f32[3328]{0:T(1024)S(1)}, f32[3328]{0:T(1024)S(1)}, f32[3328]{0:T(1024)}, f32[3328]{0:T(1024)S(1)}, /*index=5*/f32[1,1024,3328]{2,1,0:T(8,128)}) fusion(f32[1,1024,3328]{2,1,0:T(8,128)} %slice.245, f32[1,1024,6448]{2,1,0:T(8,128)} %convolution_bitcast_fusion, f32[1,1024,3328]{2,1,0:T(8,128)} %get-tuple-element.153, ...), kind=kLoop, calls=%fused_computation.12 | loop fusion | flops 68140800 | bytes 68224000 | tf_op jit(solution)/shard_map/transpose(jvp(vmap()))/reduce_sum | solution.py:67
  1183.6 17.1 broadcast_multiply_fusion
  1200.7 19.7 pad_add_fusion
  1220.4 33.2 %fusion.133 = f32[1536,6448]{0,1:T(8,128)} fusion(bf16[1,1024,1536]{2,1,0:T(8,128)(2,1)S(1)} %copy-done.30, f32[1536]{0:T(1024)S(1)} %copy-done.125, f32[1024]{0:T(1024)S(1)} %copy-done.129, f32[1,1024,3072]{2,1,0:T(8,128)} %get-tuple-element.154, f32[1,1024,3328]{2,1,0:T(8,128)} %pad_add_fusion, f32[1,1024,48]{2,1,0:T(8,128)} %get-tuple-element.136), kind=kOutput, calls=%fused_computation.176 | convolution fusion | flops 20309753856 | bytes 69183488 | tf_op jit(solution)/shard_map/dot_general | solution.py:183
  1256.3 266.5 %reduce-scatter.6.cloned.1.call-done = f32[384,6448]{0,1:T(8,128)} async-done(((f32[1536,6448]{0,1:T(8,128)}), f32[384,6448]{0,1:T(8,128)}) %reduce-scatter.6.cloned.1.call-update) | async-done | bytes 9904144 | tf_op jit(solution)/shard_map/reduce_scatter | solution.py:188
  1525.7 17.4 fusion.131
  1555.8 125.1 %all-gather.8.cloned.1.call-done = bf16[1536,6448]{0,1:T(8,128)(2,1)} async-done(((bf16[384,6448]{0,1:T(8,128)(2,1)}), bf16[1536,6448]{0,1:T(8,128)(2,1)}) %all-gather.8.cloned.1.call-update) | async-done | bytes 19808272 | tf_op jit(solution)/shard_map/all_gather | solution.py:166
  1680.9 32.1 %fusion.73 = (f32[1536]{0:T(1024)S(1)}, f32[1024]{0:T(1024)S(1)}, f32[1024,1536]{1,0:T(8,128)}) fusion(bf16[1,1024,1536]{2,1,0:T(8,128)(2,1)S(1)} %copy-done.30, f32[1024]{0:T(1024)S(1)} %copy-done.129, f32[1536]{0:T(1024)S(1)} %copy-done.125, bf16[1536,6448]{0,1:T(8,128)(2,1)} %all-gather.8.cloned.1.call-done, f32[1,1024,3072]{2,1,0:T(8,128)} %get-tuple-element.154, ...), kind=kOutput, calls=%fused_computation.116 | convolution fusion | flops 20314468352 | bytes 55676928 | tf_op jit(solution)/shard_map/dot_general | solution.py:175
  1725.1 40.2 %all-reduce.44 = (f32[384]{0:T(512)}, f32[4,832]{1,0:T(4,128)}, f32[832]{0:T(1024)}, f32[12]{0:T(128)}, f32[12]{0:T(128)}, /*index=5*/f32[12]{0:T(128)}, f32[768]{0:T(1024)}) all-reduce(f32[384]{0:T(512)S(1)} %dynamic-slice.5, f32[4,832]{1,0:T(4,128)S(1)} %copy.695, ...), channel_id=1, replica_groups=mesh['shard'=4,'rep'=8] {'rep'}, use_global_device_ids=true, to_apply=%region_59.60 | all-reduce | flops 5348 | bytes 42784 | tf_op jit(solution)/shard_map/psum | solution.py:197
  1771.7 367.8 %all-reduce.50.cloned.1.call-done = (f32[384,6448]{0,1:T(8,128)}, f32[768,1536]{1,0:T(8,128)}) async-done(((f32[384,6448]{0,1:T(8,128)}, f32[768,1536]{1,0:T(8,128)}), (f32[384,6448]{0,1:T(8,128)}, f32[768,1536]{1,0:T(8,128)})) %all-reduce.50.cloned.1.call-update) | async-done | bytes 14622736 | tf_op jit(solution)/shard_map/psum | solution.py:197
  (661 shorter events, 700.9 us)
Async XLA Ops:
  7.2 576.0 %all-gather.6.cloned.1.call-start = ((), (), s32[]{:S(2)}) async-start(), calls=%async_computation.3 | async-start | bytes 11796480 | tf_op jit(solution)/shard_map/all_gather | solution.py:128
  7.2 107.6 %collective-permute-start = (bf16[384,6448]{0,1:T(8,128)(2,1)}, bf16[384,6448]{0,1:T(8,128)(2,1)}, u32[]{:S(2)}, u32[]{:S(2)}) collective-permute-start(bf16[384,6448]{0,1:T(8,128)(2,1)} %param.13), channel_id=1, source_target_pairs={{0,8},{8,16},{16,24},{24,0},{1,9},{9,17},{17,25},{25,1},{2,10},{10... | collective-permute-start | bytes 14856200 | tf_op jit(solution)/shard_map/ppermute | solution.py:16
  7.8 261.3 %collective-permute-start.1 = (bf16[384,6448]{0,1:T(8,128)(2,1)}, bf16[384,6448]{0,1:T(8,128)(2,1)}, u32[]{:S(2)}, u32[]{:S(2)}) collective-permute-start(bf16[384,6448]{0,1:T(8,128)(2,1)} %param.13), channel_id=1, source_target_pairs={{0,24},{8,0},{16,8},{24,16},{1,25},{9,1},{17,9},{25,17},{2,26},{10... | collective-permute-start | bytes 14856200 | tf_op jit(solution)/shard_map/ppermute | solution.py:19
  114.8 159.8 %collective-permute-start.2 = (bf16[384,6448]{0,1:T(8,128)(2,1)}, bf16[384,6448]{0,1:T(8,128)(2,1)}, u32[]{:S(2)}, u32[]{:S(2)}) collective-permute-start(bf16[384,6448]{0,1:T(8,128)(2,1)} %collective-permute-done), channel_id=1, source_target_pairs={{0,8},{8,16},{16,24},{24,0},{1,9},{9,17},{17,25},{25,1},{2,10},{10... | collective-permute-start | bytes 14856200 | tf_op jit(solution)/shard_map/ppermute | solution.py:16
  117.2 1139.1 %reduce-scatter.8.cloned.1.call-start = ((), (), s32[]{:S(2)}) async-start(), calls=%async_computation.6 | async-start | bytes 23592960 | tf_op jit(solution)/shard_map/reduce_scatter | solution.py:195
  236.5 72.8 %copy-start.133 = (f32[48]{0:T(128)}, f32[48]{0:T(128)S(1)}, u32[]{:S(2)}) copy-start(f32[48]{0:T(128)S(1)} %convert_element_type.66) | copy-start | bytes 580
  452.9 323.4 %copy-start.1 = (f32[48,64,128]{2,1,0:T(8,128)}, f32[48,64,128]{2,1,0:T(8,128)S(1)}, u32[]{:S(2)}) copy-start(f32[48,64,128]{2,1,0:T(8,128)S(1)} %convolution_add_fusion) | copy-start | bytes 4718596
  458.1 300.5 %copy-start.3 = (f32[48,64,128]{2,1,0:T(8,128)}, f32[48,64,128]{2,1,0:T(8,128)S(1)}, u32[]{:S(2)}) copy-start(f32[48,64,128]{2,1,0:T(8,128)S(1)} %multiply_add_fusion.2) | copy-start | bytes 4718596
  565.8 104.8 %copy-start.44 = (f32[1,256,128]{2,1,0:T(8,128)}, f32[1,256,128]{2,1,0:T(8,128)S(1)}, u32[]{:S(2)}) copy-start(f32[1,256,128]{2,1,0:T(8,128)S(1)} %get-tuple-element.42) | copy-start | bytes 393220
  565.8 135.9 %copy-start.41 = (f32[1,256,128]{2,1,0:T(8,128)}, f32[1,256,128]{2,1,0:T(8,128)S(1)}, u32[]{:S(2)}) copy-start(f32[1,256,128]{2,1,0:T(8,128)S(1)} %get-tuple-element.54) | copy-start | bytes 393220
  583.1 939.7 %reduce-scatter.6.cloned.1.call-start = ((), (), s32[]{:S(2)}) async-start(), calls=%async_computation.5 | async-start | bytes 49520640 | tf_op jit(solution)/shard_map/reduce_scatter | solution.py:188
  1253.7 301.0 %reduce-scatter.10.cloned.1.call-start = ((), (), s32[]{:S(2)}) async-start(), calls=%async_computation.7 | async-start | bytes 2129920
  1255.6 269.8 %copy-start.118 = (f32[3072]{0:T(1024)S(1)}, f32[3072]{0:T(1024)}, u32[]{:S(2)}) copy-start(f32[3072]{0:T(1024)} %get-tuple-element.133) | copy-start | bytes 36868
  1255.6 270.0 %copy-start.136 = (f32[48]{0:T(128)S(1)}, f32[48]{0:T(128)}, u32[]{:S(2)}) copy-start(f32[48]{0:T(128)} %get-tuple-element.201) | copy-start | bytes 580
  1255.6 270.0 %copy-start.137 = (f32[48]{0:T(128)S(1)}, f32[48]{0:T(128)}, u32[]{:S(2)}) copy-start(f32[48]{0:T(128)} %get-tuple-element.199) | copy-start | bytes 580
  1255.7 270.0 %copy-start.139 = (bf16[48]{0:T(256)(128)(2,1)S(1)}, bf16[48]{0:T(256)(128)(2,1)}, u32[]{:S(2)}) copy-start(bf16[48]{0:T(256)(128)(2,1)} %copy-done.138) | copy-start | bytes 292
  1255.7 270.0 %copy-start.117 = (f32[4,1,768]{2,1,0:T(1,128)S(1)}, f32[4,1,768]{2,1,0:T(1,128)}, u32[]{:S(2)}) copy-start(f32[4,1,768]{2,1,0:T(1,128)} %convert_element_type.82) | copy-start | bytes 36868
  1255.7 270.0 %copy-start.127 = (f32[1024]{0:T(1024)S(1)}, f32[1024]{0:T(1024)}, u32[]{:S(2)}) copy-start(f32[1024]{0:T(1024)} %copy-done.126) | copy-start | bytes 12292
  1255.7 425.3 %all-gather.8.cloned.1.call-start = ((), (), s32[]{:S(2)}) async-start(), calls=%async_computation.4 | async-start | bytes 24760320 | tf_op jit(solution)/shard_map/all_gather | solution.py:166
  1256.3 883.3 %all-reduce.50.cloned.1.call-start = ((), (), s32[]{:S(2)}) async-start(), calls=%async_computation.8 | async-start | bytes 29245440 | tf_op jit(solution)/shard_map/psum | solution.py:197
  1555.8 157.3 %copy-start.98 = (f32[3328]{0:T(1024)S(1)}, f32[3328]{0:T(1024)}, u32[]{:S(2)}) copy-start(f32[3328]{0:T(1024)} %get-tuple-element.78) | copy-start | bytes 39940
  1555.8 157.3 %copy-start.130 = (f32[3072]{0:T(1024)S(1)}, f32[3072]{0:T(1024)}, u32[]{:S(2)}) copy-start(f32[3072]{0:T(1024)} %get-tuple-element.76) | copy-start | bytes 36868
  1555.8 157.3 %copy-start.135 = (f32[48]{0:T(128)S(1)}, f32[48]{0:T(128)}, u32[]{:S(2)}) copy-start(f32[48]{0:T(128)} %get-tuple-element.135) | copy-start | bytes 580
  1555.8 209.5 %copy-start.123 = (f32[1024]{0:T(1024)S(1)}, f32[1024]{0:T(1024)}, u32[]{:S(2)}) copy-start(f32[1024]{0:T(1024)} %copy-done.122) | copy-start | bytes 12292
  (130 other events, 2497.2 us)
Sparse Core Ops, SparseCore 0:
  117.4 91.3 all-gather.5
  583.2 137.3 reduce-scatter.7
  1253.8 268.9 reduce-scatter.5
  1525.8 28.7 reduce-scatter.9
  1556.1 124.8 all-gather.7
  1685.1 454.4 all-reduce.49
